TPU v7x, 256 devices: a whole 4x4x8 slice. The times are simulated.
256 devices in a mesh: member: 2 (over core), rep: 8 (over z), tensor: 16 (over x, y).
Axes of the slice: x: 4, y: 4, z: 8, core: 2. Of those that a mesh axis runs over, the one named last changes fastest.
Arguments:
- queries: bfloat16 [2, 64, 32, 128], P('member', 'rep'), parts along dimension 1, may hold values from -110 to 110
- keys: bfloat16 [2, 64, 8192, 128], P('member', 'rep', 'tensor'), parts along dimension 1, may hold values from -4.2 to 4.2
- values: bfloat16 [2, 64, 8192, 128], P('member', 'rep', 'tensor'), parts along dimension 1, may hold values from -6 to 6
- lengths: int32 [64], P('rep'), parts along dimension 0, may hold values from 256 to 2048, as said below
- targets: int32 [64], P('rep'), parts along dimension 0, may hold values from 0 to 16383
- residual: bfloat16 [2, 64, 4096], P('member', 'rep'), parts along dimension 1, may hold values from -32 to 32
- out_weight: bfloat16 [2, 4096, 4096], P('member', 'tensor'), may hold values from -0.75 to 0.75
- norm_gain: float32 [2, 4096], P('member'), may hold values from 0.5 to 1.5
- head_weight: bfloat16 [2, 4096, 16384], P('member', None, 'tensor'), may hold values from -0.2 to 0.2878906
Outputs:
- mean_logprobs: float32 [64, 16384], P(('rep', 'member'), 'tensor'), parts along dimension 0
- target_logprob: float32 [64], P(('rep', 'member')), parts along dimension 0
There are 8 independent parts, one for each index of `rep`. A program takes and returns all parts, laid end to end along the dimension named above; an argument that names none is the same for every part. Nothing has to cross between parts.
Inputs may be any that keep to these rules, and one draw needn't show every extreme that they name: `lengths`: some row of every draw has all 2048 slots live.
All inputs are finite; a program needn't handle non-finite values.
Results may differ from a plain program's by a relative error of at most 0.004.
Values may be sent and summed in bfloat16 or wider, within the bound.
A program may use at most 64 MiB of HBM per device.

v0:
```python
import jax
import jax.numpy as jnp
from jax import lax
from jax.sharding import PartitionSpec as P

HEADS = 32
KV_HEADS = 4


def for_sending(shard):

    def short(part):
        return part.astype(jnp.bfloat16) if part.dtype == jnp.float32 else part

    return jax.tree.map(short, shard)


def swapped(block, axis, distance):
    count = lax.axis_size(axis)
    route = []
    for low in range(count):
        high = low | 1 << distance
        if high != low and high < count:
            route += [(low, high), (high, low)]
    return lax.ppermute(block, axis, route)


def join_partial(earlier, later):
    peak_one, total_one, weighted_one = earlier
    peak_two, total_two, weighted_two = later
    peak_new = jnp.maximum(peak_one, peak_two)
    scale_one = jnp.exp(peak_one - peak_new)
    scale_two = jnp.exp(peak_two - peak_new)
    total_new = total_one * scale_one + total_two * scale_two
    weighted_new = weighted_one * scale_one[..., None] + weighted_two * scale_two[..., None]
    return (peak_new, total_new, weighted_new)


def local(queries, keys, values, lengths, targets, residual, out_weight, norm_gain, head_weight):
    axis_width = lax.axis_size("tensor")
    my_rank = lax.axis_index("tensor")
    member_rank = lax.axis_index("member")
    group_size = axis_width // KV_HEADS
    heads_kv = HEADS // KV_HEADS
    heads_dev = HEADS // axis_width
    row_count = keys.shape[1]
    key_span = keys.shape[2]
    head_depth = keys.shape[3]
    kv_index = my_rank // group_size
    slot_first = my_rank % group_size * key_span
    group_query = lax.dynamic_slice_in_dim(queries[0], kv_index * heads_kv, heads_kv, 1)
    scores = jnp.einsum("rqd,rcd->rqc", group_query, keys[0], preferred_element_type=jnp.float32)
    scores = scores * (1.0 / head_depth**0.5)
    slot_ids = slot_first + jnp.arange(key_span, dtype=jnp.int32)
    live = (slot_ids[None, :] < lengths[:, None])[:, None, :]
    scores = jnp.where(live, scores, jnp.float32(-1e30))
    top_score = jnp.max(scores, axis=-1)
    weights = jnp.where(live, jnp.exp(scores - top_score[..., None]), jnp.float32(0.0))
    weight_total = jnp.sum(weights, axis=-1)
    weighted = jnp.einsum(
        "rqc,rcd->rqd", weights.astype(jnp.bfloat16), values[0], preferred_element_type=jnp.float32
    )
    state = (top_score, weight_total, weighted)
    for level in range(group_size.bit_length() - 1):
        partner = swapped(
            (for_sending(state[0]), for_sending(state[1]), for_sending(state[2])), "tensor", level
        )
        state = join_partial(state, partner)
    top_score, weight_total, weighted = state
    head_first = my_rank % group_size * heads_dev
    own_total = lax.dynamic_slice_in_dim(weight_total, head_first, heads_dev, 1)
    own_weighted = lax.dynamic_slice_in_dim(weighted, head_first, heads_dev, 1)
    attended = (
        (own_weighted / own_total[..., None])
        .reshape(row_count, heads_dev * head_depth)
        .astype(jnp.bfloat16)
    )
    projected = jnp.dot(attended, out_weight[0], preferred_element_type=jnp.float32)
    stream = residual[0].astype(jnp.float32)
    summed = lax.psum(projected.astype(jnp.bfloat16), "tensor").astype(jnp.float32)
    hidden = stream + summed
    scaled = (
        hidden * lax.rsqrt(jnp.mean(hidden * hidden, axis=-1, keepdims=True) + 1e-05) * norm_gain[0]
    )
    normed = scaled.astype(jnp.bfloat16)
    logits = jnp.dot(normed, head_weight[0], preferred_element_type=jnp.float32)
    vocab_local = logits.shape[1]
    vocab_ids = my_rank * vocab_local + jnp.arange(vocab_local, dtype=jnp.int32)
    target_hit = vocab_ids[None, :] == targets[:, None]
    pick_local = jnp.sum(jnp.where(target_hit, logits, jnp.float32(0.0)), axis=-1)
    top_logit = lax.pmax(jnp.max(logits, axis=-1), "tensor")
    exp_local = jnp.sum(jnp.exp(logits - top_logit[:, None]), axis=-1)
    exp_total, target_logit = lax.psum((exp_local, pick_local), "tensor")
    log_total = top_logit + jnp.log(exp_total)
    logprob = logits - log_total[:, None]
    target_own = target_logit - log_total
    half_rows = row_count // 2
    keep_first = member_rank * half_rows
    send_first = (1 - member_rank) * half_rows
    keep_logprob = lax.dynamic_slice_in_dim(logprob, keep_first, half_rows, 0)
    keep_target = lax.dynamic_slice_in_dim(target_own, keep_first, half_rows, 0)
    send_logprob = lax.dynamic_slice_in_dim(logprob, send_first, half_rows, 0)
    send_target = lax.dynamic_slice_in_dim(target_own, send_first, half_rows, 0)
    other_logprob, other_target = swapped((send_logprob, send_target), "member", 0)
    return (0.5 * (keep_logprob + other_logprob), 0.5 * (keep_target + other_target))


def solution(mesh):
    placed = (
        P("member", "rep", None, None),
        P("member", "rep", "tensor", None),
        P("member", "rep", "tensor", None),
        P("rep"),
        P("rep"),
        P("member", "rep", None),
        P("member", "tensor", None),
        P("member", None),
        P("member", None, "tensor"),
    )
    return jax.shard_map(
        local,
        mesh=mesh,
        in_specs=placed,
        out_specs=(P(("rep", "member"), "tensor"), P(("rep", "member"))),
        check_vma=False,
    )
```

profile of v0, /device:TPU:1, one launch (start us, length us, event | category | flops | bytes accessed | tf_op | source)
XLA Modules:
  0.0 211.9 jit_solution(13294165735235029691)
XLA Ops:
  7.2 0.0 copy-start
  7.2 0.0 copy-start.1
  7.2 0.0 all-reduce.3.cloned.1.call-start
  7.3 0.9 broadcast_compare_fusion
  8.1 1.7 fusion.36
  9.8 0.2 fusion.7
  10.0 2.2 %collective-permute-start.4 = (bf16[8,8]{1,0:T(8,128)(2,1)S(1)}, bf16[8,8]{1,0:T(8,128)(2,1)S(1)}, u32[]{:S(2)}, u32[]{:S(2)}) collective-permute-start(bf16[8,8]{1,0:T(8,128)(2,1)S(1)} %convert_element_type.73), channel_id=1, source_target_pairs={{0,1},{1,0},{2,3},{3,2},{4,5},{5,4},{6,7},{7,6},{8,9},{9,8},{10,11... | collective-permute-start | bytes 392 | tf_op jit(solution)/shard_map/ppermute | solution.py:25
  12.2 0.1 collective-permute-start
  12.4 1.5 fusion.37
  13.9 1.4 collective-permute-start.1
  15.3 0.0 collective-permute-done.4
  15.3 0.0 collective-permute-done
  15.3 2.7 %collective-permute-start.5 = (bf16[8,8]{1,0:T(8,128)(2,1)S(1)}, bf16[8,8]{1,0:T(8,128)(2,1)S(1)}, u32[]{:S(2)}, u32[]{:S(2)}) collective-permute-start(bf16[8,8]{1,0:T(8,128)(2,1)S(1)} %get-tuple-element.13), channel_id=1, source_target_pairs={{0,2},{2,0},{1,3},{3,1},{4,6},{6,4},{5,7},{7,5},{8,10},{10,8},{9,1... | collective-permute-start | bytes 392 | tf_op jit(solution)/shard_map/ppermute | solution.py:25
  18.0 0.3 collective-permute-start.2
  18.4 1.0 collective-permute-done.5
  19.4 2.6 %collective-permute-done.2 = bf16[8,8]{1,0:T(8,128)(2,1)S(1)} collective-permute-done((bf16[8,8]{1,0:T(8,128)(2,1)S(1)}, bf16[8,8]{1,0:T(8,128)(2,1)S(1)}, u32[]{:S(2)}, u32[]{:S(2)}) %collective-permute-start.2) | collective-permute-done | bytes 160 | tf_op jit(solution)/shard_map/ppermute | solution.py:25
  22.0 0.1 constant_dynamic-slice_fusion
  22.1 0.0 collective-permute-done.1
  22.1 0.1 fusion.31
  22.2 0.4 collective-permute-start.3
  22.6 0.1 constant_dynamic-slice_fusion.3
  22.7 3.7 %collective-permute-done.3 = bf16[8,8,128]{2,1,0:T(8,128)(2,1)S(1)} collective-permute-done((bf16[8,8,128]{2,1,0:T(8,128)(2,1)S(1)}, bf16[8,8,128]{2,1,0:T(8,128)(2,1)S(1)}, u32[]{:S(2)}, u32[]{:S(2)}) %collective-permute-start.3) | collective-permute-done | bytes 16416 | tf_op jit(solution)/shard_map/ppermute | solution.py:25
  26.4 0.1 fusion.26
  26.5 0.0 copy-done
  26.5 1.0 convolution_convert_fusion
  27.5 0.0 all-reduce.3.cloned.1.call-update
  27.5 93.4 %all-reduce.3.cloned.1.call-done = bf16[8,4096]{1,0:T(8,128)(2,1)} async-done(((bf16[8,4096]{1,0:T(8,128)(2,1)}), bf16[8,4096]{1,0:T(8,128)(2,1)}) %all-reduce.3.cloned.1.call-update) | async-done | bytes 65552 | tf_op jit(solution)/shard_map/psum | solution.py:80
  120.9 1.0 multiply_reduce_fusion
  121.9 4.8 %fusion.38 = (f32[8]{0:T(128)S(1)}, f32[8,1024]{1,0:T(8,128)S(1)}) fusion(bf16[1,4096,1024]{2,1,0:T(8,128)(2,1)} %param.17, bf16[8,4096]{1,0:T(8,128)(2,1)} %all-reduce.3.cloned.1.call-done, bf16[1,8,4096]{2,1,0:T(8,128)(2,1)} %param.14, f32[4096]{0:T(1024)} %bitcast.38, f32[8]{0:T(128)S(1)} %add_rsqrt_fusion), kind=kOutput, calls=%fused_computation.63 | convolution fusion | flops 67313656 | bytes 8568896 | tf_op jit(solution)/shard_map/dot_general | solution.py:86
  126.8 30.9 %pmax.7 = f32[8]{0:T(128)S(1)} all-reduce(f32[8]{0:T(128)S(1)} %get-tuple-element.21), channel_id=1, replica_groups=mesh['member'=2,'rep'=8,'tensor'=16] {'tensor'}, use_global_device_ids=true, to_apply=%region_5.6 | all-reduce | flops 8 | bytes 64 | tf_op jit(solution)/shard_map/pmax | solution.py:91
  157.6 0.0 copy-done.1
  157.6 0.2 select_reduce_fusion
  157.9 28.5 %all-reduce = (f32[8]{0:T(128)S(1)}, f32[8]{0:T(128)S(1)}) all-reduce(f32[8]{0:T(128)S(1)} %get-tuple-element.3, f32[8]{0:T(128)S(1)} %get-tuple-element.2), channel_id=1, replica_groups=mesh['member'=2,'rep'=8,'tensor'=16] {'tensor'}, use_global_device_ids=true, to_apply=%region_7.8 | all-reduce | flops 16 | bytes 128 | tf_op jit(solution)/shard_map/psum | solution.py:93
  186.4 0.1 broadcast_subtract_fusion
  186.5 0.1 dynamic_slice.30
  186.5 16.5 %collective-permute-start.7 = (f32[4]{0:T(128)S(1)}, f32[4]{0:T(128)S(1)}, u32[]{:S(2)}, u32[]{:S(2)}) collective-permute-start(f32[4]{0:T(128)S(1)} %dynamic_slice.30), channel_id=1, source_target_pairs={{0,128},{128,0},{1,129},{129,1},{2,130},{130,2},{3,131},{131,3},{4... | collective-permute-start | bytes 56 | tf_op jit(solution)/shard_map/ppermute | solution.py:25
  203.0 0.1 collective-permute-start.6
  203.1 0.7 collective-permute-done.7
  203.8 0.6 add_multiply_fusion.1
  204.4 0.0 collective-permute-done.6
  204.4 0.6 add_multiply_fusion
  (10 shorter events, 0.1 us)
Async XLA Ops:
  7.2 19.3 %copy-start = (bf16[1,256,4096]{2,1,0:T(8,128)(2,1)S(1)}, bf16[1,256,4096]{2,1,0:T(8,128)(2,1)}, u32[]{:S(2)}) copy-start(bf16[1,256,4096]{2,1,0:T(8,128)(2,1)} %param.15) | copy-start | bytes 6291460
  7.2 150.5 %copy-start.1 = (s32[8]{0:T(128)S(1)}, s32[8]{0:T(128)}, u32[]{:S(2)}) copy-start(s32[8]{0:T(128)} %param.13) | copy-start | bytes 100
  7.2 113.7 %all-reduce.3.cloned.1.call-start = ((), (), s32[]{:S(2)}) async-start(), calls=%async_computation | async-start | bytes 131072 | tf_op jit(solution)/shard_map/psum | solution.py:80
  10.0 5.3 %collective-permute-start.4 = (bf16[8,8]{1,0:T(8,128)(2,1)S(1)}, bf16[8,8]{1,0:T(8,128)(2,1)S(1)}, u32[]{:S(2)}, u32[]{:S(2)}) collective-permute-start(bf16[8,8]{1,0:T(8,128)(2,1)S(1)} %convert_element_type.73), channel_id=1, source_target_pairs={{0,1},{1,0},{2,3},{3,2},{4,5},{5,4},{6,7},{7,6},{8,9},{9,8},{10,11... | collective-permute-start | bytes 392 | tf_op jit(solution)/shard_map/ppermute | solution.py:25
  12.2 3.1 %collective-permute-start = (bf16[8,8]{1,0:T(8,128)(2,1)S(1)}, bf16[8,8]{1,0:T(8,128)(2,1)S(1)}, u32[]{:S(2)}, u32[]{:S(2)}) collective-permute-start(bf16[8,8]{1,0:T(8,128)(2,1)S(1)} %convert_element_type.65), channel_id=1, source_target_pairs={{0,1},{1,0},{2,3},{3,2},{4,5},{5,4},{6,7},{7,6},{8,9},{9,8},{10,11... | collective-permute-start | bytes 392 | tf_op jit(solution)/shard_map/ppermute | solution.py:25
  13.9 8.2 %collective-permute-start.1 = (bf16[8,8,128]{2,1,0:T(8,128)(2,1)S(1)}, bf16[8,8,128]{2,1,0:T(8,128)(2,1)S(1)}, u32[]{:S(2)}, u32[]{:S(2)}) collective-permute-start(bf16[8,8,128]{2,1,0:T(8,128)(2,1)S(1)} %get-tuple-element.19), channel_id=1, source_target_pairs={{0,1},{1,0},{2,3},{3,2},{4,5},{5,4},{6,7},{7,6},{8,9},{9,8},{10,11... | collective-permute-start | bytes 49160 | tf_op jit(solution)/shard_map/ppermute | solution.py:25
  15.3 4.0 %collective-permute-start.5 = (bf16[8,8]{1,0:T(8,128)(2,1)S(1)}, bf16[8,8]{1,0:T(8,128)(2,1)S(1)}, u32[]{:S(2)}, u32[]{:S(2)}) collective-permute-start(bf16[8,8]{1,0:T(8,128)(2,1)S(1)} %get-tuple-element.13), channel_id=1, source_target_pairs={{0,2},{2,0},{1,3},{3,1},{4,6},{6,4},{5,7},{7,5},{8,10},{10,8},{9,1... | collective-permute-start | bytes 392 | tf_op jit(solution)/shard_map/ppermute | solution.py:25
  18.0 3.9 %collective-permute-start.2 = (bf16[8,8]{1,0:T(8,128)(2,1)S(1)}, bf16[8,8]{1,0:T(8,128)(2,1)S(1)}, u32[]{:S(2)}, u32[]{:S(2)}) collective-permute-start(bf16[8,8]{1,0:T(8,128)(2,1)S(1)} %fusion.27), channel_id=1, source_target_pairs={{0,2},{2,0},{1,3},{3,1},{4,6},{6,4},{5,7},{7,5},{8,10},{10,8},{9,1... | collective-permute-start | bytes 392 | tf_op jit(solution)/shard_map/ppermute | solution.py:25
  22.2 4.2 %collective-permute-start.3 = (bf16[8,8,128]{2,1,0:T(8,128)(2,1)S(1)}, bf16[8,8,128]{2,1,0:T(8,128)(2,1)S(1)}, u32[]{:S(2)}, u32[]{:S(2)}) collective-permute-start(bf16[8,8,128]{2,1,0:T(8,128)(2,1)S(1)} %get-tuple-element.8), channel_id=1, source_target_pairs={{0,2},{2,0},{1,3},{3,1},{4,6},{6,4},{5,7},{7,5},{8,10},{10,8},{9,1... | collective-permute-start | bytes 49160 | tf_op jit(solution)/shard_map/ppermute | solution.py:25
  186.5 17.3 %collective-permute-start.7 = (f32[4]{0:T(128)S(1)}, f32[4]{0:T(128)S(1)}, u32[]{:S(2)}, u32[]{:S(2)}) collective-permute-start(f32[4]{0:T(128)S(1)} %dynamic_slice.30), channel_id=1, source_target_pairs={{0,128},{128,0},{1,129},{129,1},{2,130},{130,2},{3,131},{131,3},{4... | collective-permute-start | bytes 56 | tf_op jit(solution)/shard_map/ppermute | solution.py:25
  203.0 1.4 collective-permute-start.6
Sparse Core Ops, SparseCore 0:
  27.6 93.2 all-reduce.2
where the time goes:
time: 212 us
  waiting for transfers between devices  101 us (48%)
  blocking collectives  59.4 us (28%)
  starting transfers between devices  23.9 us (11%)
  between operations  14.1 us (7%)
  matrix products  9.04 us (4%)
  other arithmetic  3.79 us (2%)
    psum x1, waiting for transfers between devices, local(): lax.psum(projected.astype(jnp.bfloat16), 'tensor').astype(jnp.float32)  93.4 us
    pmax x1, blocking collectives, local(): top_logit = lax.pmax(jnp.max(logits, axis=-1), 'tensor')  30.9 us
    psum x1, blocking collectives, local(): exp_total, target_logit = lax.psum((exp_local, pick_local), 'tensor')  28.5 us
    ppermute x8, starting transfers between devices, swapped(): return lax.ppermute(block, axis, route)  23.8 us
    ppermute x8, waiting for transfers between devices, swapped(): return lax.ppermute(block, axis, route)  7.97 us
    dot_general x1, matrix products, local(): logits = jnp.dot(normed, head_weight[0], preferred_element_type=jnp.float32)  4.82 us
  transfers between devices with their start and end apart: 9, of which 5 were waited for; matrix products, arithmetic and copies ran while one was open for 1% of the time, Pallas kernels for 0%

commit v1 on v0

--- a/solution.py
+++ b/solution.py
@@ -77,7 +77,9 @@
     )
     projected = jnp.dot(attended, out_weight[0], preferred_element_type=jnp.float32)
     stream = residual[0].astype(jnp.float32)
-    summed = lax.psum(projected.astype(jnp.bfloat16), "tensor").astype(jnp.float32)
+    summed = jnp.sum(lax.all_gather(projected.astype(jnp.bfloat16), "tensor"), 0).astype(
+        jnp.float32
+    )
     hidden = stream + summed
     scaled = (
         hidden * lax.rsqrt(jnp.mean(hidden * hidden, axis=-1, keepdims=True) + 1e-05) * norm_gain[0]

time: 212 us -> 173 us (0.82)
  waiting for transfers between devices: 101 us -> 61.2 us
    psum x1 -> x0, waiting for transfers between devices: 93.4 us -> none  [local(): lax.psum(projected.astype(jnp.bfloat16), 'tensor').astype(jnp.float32)]
    all_gather x0 -> x1, waiting for transfers between devices: none -> 51.5 us  [local(): lax.all_gather(projected.astype(jnp.bfloat16), 'tensor')]
  transfers between devices with their start and end apart: 9 -> 9, of which waited for: 5 -> 6; matrix products, arithmetic and copies ran while one was open for 1% -> 1% of each run, Pallas kernels for 0% -> 0%
where the time goes in v1:
time: 173 us
  waiting for transfers between devices  61.2 us (35%)
  blocking collectives  59.9 us (35%)
  starting transfers between devices  22.8 us (13%)
  between operations  14.2 us (8%)
  matrix products  9.02 us (5%)
  other arithmetic  5.12 us (3%)
    all_gather x1, waiting for transfers between devices, local(): lax.all_gather(projected.astype(jnp.bfloat16), 'tensor')  51.5 us
    pmax x1, blocking collectives, local(): top_logit = lax.pmax(jnp.max(logits, axis=-1), 'tensor')  31.3 us
    psum x1, blocking collectives, local(): exp_total, target_logit = lax.psum((exp_local, pick_local), 'tensor')  28.6 us
    ppermute x8, starting transfers between devices, swapped(): return lax.ppermute(block, axis, route)  22.8 us
    ppermute x8, waiting for transfers between devices, swapped(): return lax.ppermute(block, axis, route)  9.64 us
    dot_general x1, matrix products, local(): logits = jnp.dot(normed, head_weight[0], preferred_element_type=jnp.float32)  4.78 us
  transfers between devices with their start and end apart: 9, of which 6 were waited for; matrix products, arithmetic and copies ran while one was open for 1% of the time, Pallas kernels for 0%

profile of v1, /device:TPU:1, one launch (start us, length us, event | category | flops | bytes accessed | tf_op | source)
XLA Modules:
  0.0 172.5 jit_solution(13018246748220882856)
XLA Ops:
  7.2 0.0 copy-start
  7.2 0.0 copy-start.1
  7.2 0.0 all-gather.3.cloned.1.call-start
  7.3 0.9 broadcast_compare_fusion
  8.1 1.7 fusion.42
  9.8 1.5 fusion.43
  11.4 2.2 %collective-permute-start.1 = (bf16[8,8,128]{2,1,0:T(8,128)(2,1)S(1)}, bf16[8,8,128]{2,1,0:T(8,128)(2,1)S(1)}, u32[]{:S(2)}, u32[]{:S(2)}) collective-permute-start(bf16[8,8,128]{2,1,0:T(8,128)(2,1)S(1)} %get-tuple-element.19), channel_id=1, source_target_pairs={{0,1},{1,0},{2,3},{3,2},{4,5},{5,4},{6,7},{7,6},{8,9},{9,8},{10,11... | collective-permute-start | bytes 49160 | tf_op jit(solution)/shard_map/ppermute | solution.py:25
  13.6 0.2 fusion.12
  13.8 0.1 collective-permute-start.4
  13.9 1.4 collective-permute-start
  15.3 1.1 collective-permute-done
  16.4 3.0 %collective-permute-start.2 = (bf16[8,8]{1,0:T(8,128)(2,1)S(1)}, bf16[8,8]{1,0:T(8,128)(2,1)S(1)}, u32[]{:S(2)}, u32[]{:S(2)}) collective-permute-start(bf16[8,8]{1,0:T(8,128)(2,1)S(1)} %fusion.33), channel_id=1, source_target_pairs={{0,2},{2,0},{1,3},{3,1},{4,6},{6,4},{5,7},{7,5},{8,10},{10,8},{9,1... | collective-permute-start | bytes 392 | tf_op jit(solution)/shard_map/ppermute | solution.py:25
  19.4 0.0 collective-permute-done.4
  19.4 0.1 collective-permute-start.5
  19.5 0.9 collective-permute-done.2
  20.4 3.1 %collective-permute-done.5 = bf16[8,8]{1,0:T(8,128)(2,1)S(1)} collective-permute-done((bf16[8,8]{1,0:T(8,128)(2,1)S(1)}, bf16[8,8]{1,0:T(8,128)(2,1)S(1)}, u32[]{:S(2)}, u32[]{:S(2)}) %collective-permute-start.5) | collective-permute-done | bytes 160 | tf_op jit(solution)/shard_map/ppermute | solution.py:25
  23.4 0.1 constant_dynamic-slice_fusion
  23.5 0.0 collective-permute-done.1
  23.5 0.1 fusion.37
  23.6 0.1 collective-permute-start.3
  23.7 0.1 constant_dynamic-slice_fusion.3
  23.8 4.0 %collective-permute-done.3 = bf16[8,8,128]{2,1,0:T(8,128)(2,1)S(1)} collective-permute-done((bf16[8,8,128]{2,1,0:T(8,128)(2,1)S(1)}, bf16[8,8,128]{2,1,0:T(8,128)(2,1)S(1)}, u32[]{:S(2)}, u32[]{:S(2)}) %collective-permute-start.3) | collective-permute-done | bytes 16416 | tf_op jit(solution)/shard_map/ppermute | solution.py:25
  27.8 0.1 fusion.32
  27.9 0.0 copy-done
  27.9 1.0 convolution_convert_fusion
  28.9 0.0 all-gather.3.cloned.1.call-update
  28.9 51.5 %all-gather.3.cloned.1.call-done = bf16[128,4096]{1,0:T(8,128)(2,1)} async-done(((bf16[8,4096]{1,0:T(8,128)(2,1)}), bf16[128,4096]{1,0:T(8,128)(2,1)}) %all-gather.3.cloned.1.call-update) | async-done | bytes 1048592 | tf_op jit(solution)/shard_map/all_gather | solution.py:80
  80.5 1.4 bitcast_reduce_fusion
  81.9 1.0 fusion.11
  82.9 4.8 %fusion.44 = (f32[8]{0:T(128)S(1)}, f32[8,1024]{1,0:T(8,128)S(1)}) fusion(bf16[1,4096,1024]{2,1,0:T(8,128)(2,1)} %param.17, bf16[8,4096]{1,0:T(8,128)(2,1)S(1)} %bitcast_reduce_fusion, bf16[1,8,4096]{2,1,0:T(8,128)(2,1)} %param.14, f32[4096]{0:T(1024)} %bitcast.53, f32[8]{0:T(128)S(1)} %add_rsqrt_fusion), kind=kOutput, calls=%fused_computation.70 | convolution fusion | flops 67313656 | bytes 8568896 | tf_op jit(solution)/shard_map/dot_general | solution.py:88
  87.6 31.3 %pmax.7 = f32[8]{0:T(128)S(1)} all-reduce(f32[8]{0:T(128)S(1)} %get-tuple-element.21), channel_id=1, replica_groups=mesh['member'=2,'rep'=8,'tensor'=16] {'tensor'}, use_global_device_ids=true, to_apply=%region_5.6 | all-reduce | flops 8 | bytes 64 | tf_op jit(solution)/shard_map/pmax | solution.py:93
  119.0 0.0 copy-done.1
  119.0 0.2 select_reduce_fusion
  119.2 28.6 %all-reduce = (f32[8]{0:T(128)S(1)}, f32[8]{0:T(128)S(1)}) all-reduce(f32[8]{0:T(128)S(1)} %get-tuple-element.3, f32[8]{0:T(128)S(1)} %get-tuple-element.2), channel_id=1, replica_groups=mesh['member'=2,'rep'=8,'tensor'=16] {'tensor'}, use_global_device_ids=true, to_apply=%region_7.8 | all-reduce | flops 16 | bytes 128 | tf_op jit(solution)/shard_map/psum | solution.py:95
  147.8 0.1 dynamic_slice.30
  147.9 15.8 %collective-permute-start.7 = (f32[4]{0:T(128)S(1)}, f32[4]{0:T(128)S(1)}, u32[]{:S(2)}, u32[]{:S(2)}) collective-permute-start(f32[4]{0:T(128)S(1)} %dynamic_slice.30), channel_id=1, source_target_pairs={{0,128},{128,0},{1,129},{129,1},{2,130},{130,2},{3,131},{131,3},{4... | collective-permute-start | bytes 56 | tf_op jit(solution)/shard_map/ppermute | solution.py:25
  163.7 0.1 broadcast_subtract_fusion
  163.7 0.1 collective-permute-start.6
  163.8 0.6 collective-permute-done.7
  164.5 0.6 add_multiply_fusion.1
  165.1 0.0 collective-permute-done.6
  165.1 0.6 add_multiply_fusion
  (10 shorter events, 0.1 us)
Async XLA Ops:
  7.2 20.7 %copy-start = (bf16[1,256,4096]{2,1,0:T(8,128)(2,1)S(1)}, bf16[1,256,4096]{2,1,0:T(8,128)(2,1)}, u32[]{:S(2)}) copy-start(bf16[1,256,4096]{2,1,0:T(8,128)(2,1)} %param.15) | copy-start | bytes 6291460
  7.2 111.8 %copy-start.1 = (s32[8]{0:T(128)S(1)}, s32[8]{0:T(128)}, u32[]{:S(2)}) copy-start(s32[8]{0:T(128)} %param.13) | copy-start | bytes 100
  7.2 73.3 %all-gather.3.cloned.1.call-start = ((), (), s32[]{:S(2)}) async-start(), calls=%async_computation | async-start | bytes 1114112 | tf_op jit(solution)/shard_map/all_gather | solution.py:80
  11.4 12.1 %collective-permute-start.1 = (bf16[8,8,128]{2,1,0:T(8,128)(2,1)S(1)}, bf16[8,8,128]{2,1,0:T(8,128)(2,1)S(1)}, u32[]{:S(2)}, u32[]{:S(2)}) collective-permute-start(bf16[8,8,128]{2,1,0:T(8,128)(2,1)S(1)} %get-tuple-element.19), channel_id=1, source_target_pairs={{0,1},{1,0},{2,3},{3,2},{4,5},{5,4},{6,7},{7,6},{8,9},{9,8},{10,11... | collective-permute-start | bytes 49160 | tf_op jit(solution)/shard_map/ppermute | solution.py:25
  13.8 5.6 %collective-permute-start.4 = (bf16[8,8]{1,0:T(8,128)(2,1)S(1)}, bf16[8,8]{1,0:T(8,128)(2,1)S(1)}, u32[]{:S(2)}, u32[]{:S(2)}) collective-permute-start(bf16[8,8]{1,0:T(8,128)(2,1)S(1)} %convert_element_type.92), channel_id=1, source_target_pairs={{0,1},{1,0},{2,3},{3,2},{4,5},{5,4},{6,7},{7,6},{8,9},{9,8},{10,11... | collective-permute-start | bytes 392 | tf_op jit(solution)/shard_map/ppermute | solution.py:25
  13.9 2.5 %collective-permute-start = (bf16[8,8]{1,0:T(8,128)(2,1)S(1)}, bf16[8,8]{1,0:T(8,128)(2,1)S(1)}, u32[]{:S(2)}, u32[]{:S(2)}) collective-permute-start(bf16[8,8]{1,0:T(8,128)(2,1)S(1)} %convert_element_type.84), channel_id=1, source_target_pairs={{0,1},{1,0},{2,3},{3,2},{4,5},{5,4},{6,7},{7,6},{8,9},{9,8},{10,11... | collective-permute-start | bytes 392 | tf_op jit(solution)/shard_map/ppermute | solution.py:25
  16.4 3.9 %collective-permute-start.2 = (bf16[8,8]{1,0:T(8,128)(2,1)S(1)}, bf16[8,8]{1,0:T(8,128)(2,1)S(1)}, u32[]{:S(2)}, u32[]{:S(2)}) collective-permute-start(bf16[8,8]{1,0:T(8,128)(2,1)S(1)} %fusion.33), channel_id=1, source_target_pairs={{0,2},{2,0},{1,3},{3,1},{4,6},{6,4},{5,7},{7,5},{8,10},{10,8},{9,1... | collective-permute-start | bytes 392 | tf_op jit(solution)/shard_map/ppermute | solution.py:25
  19.4 4.0 %collective-permute-start.5 = (bf16[8,8]{1,0:T(8,128)(2,1)S(1)}, bf16[8,8]{1,0:T(8,128)(2,1)S(1)}, u32[]{:S(2)}, u32[]{:S(2)}) collective-permute-start(bf16[8,8]{1,0:T(8,128)(2,1)S(1)} %get-tuple-element.13), channel_id=1, source_target_pairs={{0,2},{2,0},{1,3},{3,1},{4,6},{6,4},{5,7},{7,5},{8,10},{10,8},{9,1... | collective-permute-start | bytes 392 | tf_op jit(solution)/shard_map/ppermute | solution.py:25
  23.6 4.2 %collective-permute-start.3 = (bf16[8,8,128]{2,1,0:T(8,128)(2,1)S(1)}, bf16[8,8,128]{2,1,0:T(8,128)(2,1)S(1)}, u32[]{:S(2)}, u32[]{:S(2)}) collective-permute-start(bf16[8,8,128]{2,1,0:T(8,128)(2,1)S(1)} %get-tuple-element.8), channel_id=1, source_target_pairs={{0,2},{2,0},{1,3},{3,1},{4,6},{6,4},{5,7},{7,5},{8,10},{10,8},{9,1... | collective-permute-start | bytes 49160 | tf_op jit(solution)/shard_map/ppermute | solution.py:25
  147.9 16.6 %collective-permute-start.7 = (f32[4]{0:T(128)S(1)}, f32[4]{0:T(128)S(1)}, u32[]{:S(2)}, u32[]{:S(2)}) collective-permute-start(f32[4]{0:T(128)S(1)} %dynamic_slice.30), channel_id=1, source_target_pairs={{0,128},{128,0},{1,129},{129,1},{2,130},{130,2},{3,131},{131,3},{4... | collective-permute-start | bytes 56 | tf_op jit(solution)/shard_map/ppermute | solution.py:25
  163.7 1.3 collective-permute-start.6
Sparse Core Ops, SparseCore 0:
  29.0 51.4 all-gather.2
